TPU v7x, 32 devices: a whole 2x2x4 slice. The times are simulated.
32 devices in a mesh: gx: 4 (over y, x), gy: 4 (over z), gz: 2 (over core).
Axes of the slice: x: 2, y: 2, z: 4, core: 2. Of those that a mesh axis runs over, the one named last changes fastest.
Arguments:
- right_side: float32 [16, 256, 512], P('gz', 'gx', 'gy'), may hold values from -6 to 6
- permeability: float32 [16, 256, 512], P('gz', 'gx', 'gy'), may hold values from 0.05 to 50
- storage: float32 [16, 256, 512], P('gz', 'gx', 'gy'), may hold values from 0.05 to 0.5
- deflation: float32 [8, 16, 256, 512], P(None, 'gz', 'gx', 'gy'), may hold values from -0.0234375 to 0.0234375
- coarse_inverse: float32 [256, 256], P('gx'), as said below
- owners: int32 [2, 4, 4, 8], P('gz', 'gx', 'gy'), may hold values from 0 to 255, as said below
- margin: int32 [2, 4, 4, 6], P('gz', 'gx', 'gy'), may hold values from 0 to 1
Outputs:
- solution: float32 [16, 256, 512], P('gz', 'gx', 'gy')
- residual: float32 [16, 256, 512], P('gz', 'gx', 'gy')
Inputs may be any that keep to these rules, and one draw needn't show every extreme that they name: `coarse_inverse`: symmetric and positive definite. `owners`: every coarse index appears exactly once.
All inputs are finite; a program needn't handle non-finite values.
Results may differ from a plain program's by a relative error of at most 0.0003.
Values sent between devices are 32-bit elements; how exact they have to be, the bound alone decides.
No kernel may reach another device: no remote copies, remote signals or barrier semaphores. Data moves between devices by JAX's collectives and lax.ppermute only.
A program may use at most 128 MiB of HBM per device.

v0:
```python
import jax
import jax.numpy as jnp
from jax import lax
from jax.sharding import PartitionSpec as P

ITERS = 4
RELAXATION = 0.7
PRECISE = lax.Precision.HIGHEST


def padded_2(cells, sides, width):
    for axis, dim in sides:
        count = lax.axis_size(axis)
        ends = count - 1
        head = lax.slice_in_dim(cells, 0, width, axis=dim)
        tail = lax.slice_in_dim(cells, cells.shape[dim] - width, cells.shape[dim], axis=dim)
        cells = jnp.concatenate(
            [
                lax.ppermute(tail, axis, [(i, (i + 1) % count) for i in range(ends)]),
                cells,
                lax.ppermute(head, axis, [((i + 1) % count, i) for i in range(ends)]),
            ],
            axis=dim,
        )
    return cells


def conduct(first_perm, second_perm):
    return 2.0 * first_perm * second_perm / jnp.maximum(first_perm + second_perm, 0.05)


def neighbour(padded, dimension, offset):
    starts = [1, 1, 1]
    starts[dimension] = 1 + offset
    limits = [
        starts[0] + padded.shape[0] - 2,
        starts[1] + padded.shape[1] - 2,
        starts[2] + padded.shape[2] - 2,
    ]
    return lax.slice(padded, starts, limits)


def diagonal_of(perm_pad, storage_in):
    perm_center = neighbour(perm_pad, 0, 0)
    diagonal = storage_in
    for dimension in range(3):
        for offset in (-1, 1):
            diagonal = diagonal + conduct(perm_center, neighbour(perm_pad, dimension, offset))
    return diagonal


def stencil(padded, perm_pad, storage_in):
    center = neighbour(padded, 0, 0)
    perm_center = neighbour(perm_pad, 0, 0)
    applied = storage_in * center
    for dimension in range(3):
        for offset in (-1, 1):
            transmit = conduct(perm_center, neighbour(perm_pad, dimension, offset))
            applied = applied + transmit * (center - neighbour(padded, dimension, offset))
    return applied


def line_mask(length, low_side, high_side, position, blocks):
    places = jnp.arange(length + 2, dtype=jnp.int32)
    inside = (places >= 1 - low_side) & (places <= length + high_side)
    ingrid = ((places >= 1) | (position > 0)) & ((places <= length) | (position < blocks - 1))
    return (inside & ingrid).astype(jnp.float32)


def local_solve(residual_ext, perm_pad, storage_ext, keep_mask, inverse):
    source = keep_mask * residual_ext
    solved = RELAXATION * inverse * source
    applied = stencil(jnp.pad(solved, 1), perm_pad, storage_ext)
    solved = solved + RELAXATION * inverse * (source - applied)
    return solved[1:-1, 1:-1, 1:-1]


def local(right_side, permeability, storage, deflation, coarse_inverse, owners, margin):
    widened = padded_2(jnp.stack((permeability, storage)), (("gx", 2), ("gy", 3), ("gz", 1)), 2)
    perm_wide = widened[0]
    perm_near = perm_wide[1:-1, 1:-1, 1:-1]
    storage_ext = widened[1][1:-1, 1:-1, 1:-1]
    local_z, local_x, local_y = right_side.shape
    depths = margin.reshape(6)
    keep_mask = (
        line_mask(local_z, depths[0], depths[1], lax.axis_index("gz"), lax.axis_size("gz"))[
            :, None, None
        ]
        * line_mask(local_x, depths[2], depths[3], lax.axis_index("gx"), lax.axis_size("gx"))[
            None, :, None
        ]
        * line_mask(local_y, depths[4], depths[5], lax.axis_index("gy"), lax.axis_size("gy"))[
            None, None, :
        ]
    )
    diagonal = diagonal_of(perm_wide, storage_ext)
    inverse = keep_mask / jnp.where(keep_mask > 0, diagonal, 1.0)
    flat_vectors = deflation.reshape(deflation.shape[0], -1)
    order_total = coarse_inverse.shape[1]
    owner_list = owners.reshape(-1)
    picker = (owner_list[:, None] == jnp.arange(order_total, dtype=jnp.int32)[None, :]).astype(
        jnp.float32
    )

    def coarse_terms(field):
        coefficients = jnp.dot(flat_vectors, field.reshape(-1), precision=PRECISE)
        return jnp.dot(coefficients, picker, precision=PRECISE)

    def coarse_field(vector):
        solved_part = jnp.dot(coarse_inverse, vector, precision=PRECISE)
        solved = lax.all_gather(solved_part, "gx", axis=0, tiled=True)
        picked = jnp.dot(picker, solved, precision=PRECISE)
        return jnp.dot(picked, flat_vectors, precision=PRECISE).reshape(right_side.shape)

    def residual_rim(residual):
        return padded_2(residual, (("gx", 1), ("gy", 2), ("gz", 0)), 1)

    def precondition(residual_ext, vector):
        return local_solve(residual_ext, perm_wide, storage_ext, keep_mask, inverse) + coarse_field(
            vector
        )

    def inner_of(residual, precond):
        return lax.psum(jnp.sum(residual * precond), ("gx", "gy", "gz"))

    solution = jnp.zeros(right_side.shape, jnp.float32)
    residual = right_side
    residual_ext = residual_rim(residual)
    vector = lax.psum(coarse_terms(residual), ("gx", "gy", "gz"))
    precond = precondition(residual_ext, vector)
    inner_prod = inner_of(residual, precond)
    direction = precond
    for iteration in range(ITERS):
        padded = padded_2(direction, (("gx", 1), ("gy", 2), ("gz", 0)), 1)
        applied = stencil(padded, perm_near, storage)
        curvature, coarse_image = lax.psum(
            (jnp.sum(direction * applied), coarse_terms(applied)), ("gx", "gy", "gz")
        )
        step_size = inner_prod / curvature
        solution = solution + step_size * direction
        residual = residual - step_size * applied
        if iteration + 1 < ITERS:
            residual_ext = residual_rim(residual)
            vector = vector - step_size * coarse_image
            precond = precondition(residual_ext, vector)
            fresh_prod = inner_of(residual, precond)
            direction = precond + fresh_prod / inner_prod * direction
            inner_prod = fresh_prod
    return (solution, residual)


def solution(mesh):
    in_specs = (
        P("gz", "gx", "gy"),
        P("gz", "gx", "gy"),
        P("gz", "gx", "gy"),
        P(None, "gz", "gx", "gy"),
        P("gx", None),
        P("gz", "gx", "gy", None),
        P("gz", "gx", "gy", None),
    )
    out_specs = (P("gz", "gx", "gy"), P("gz", "gx", "gy"))
    return jax.shard_map(local, mesh=mesh, in_specs=in_specs, out_specs=out_specs, check_vma=False)
```

profile of v0, /device:TPU:0, one launch (start us, length us, event | category | flops | bytes accessed | tf_op | source)
XLA Modules:
  0.0 727.6 jit_solution(15111064473556556727)
XLA Ops:
  2.1 4.9 collective-permute-start
  16.8 6.5 fusion.8
  23.5 42.0 %psum.84 = f32[256]{0:T(256)S(1)} all-reduce(f32[256]{0:T(256)S(1)} %bitcast.151), channel_id=1, replica_groups=mesh['gx'=4,'gy'=4,'gz'=2] {'gx','gy','gz'}, use_global_device_ids=true, to_apply=%region_0.1 | all-reduce | flops 256 | bytes 2048 | tf_op jit(solution)/shard_map/psum | solution.py:129
  67.2 11.1 %all-reduce.4 = f32[256]{0:T(256)S(1)} all-reduce(f32[256]{0:T(256)S(1)} %dynamic-update-slice), channel_id=1, replica_groups=mesh['gx'=4,'gy'=4,'gz'=2] {'gx'}, use_global_device_ids=true, to_apply=%add.4 | all-reduce | flops 256 | bytes 2048
  95.5 5.1 collective-permute-start.2
  123.9 6.1 fusion.144
  130.0 8.2 %multiply_add_fusion.3 = (f32[10,66,130]{2,0,1:T(8,128)}, f32[10,66,130]{2,0,1:T(8,128)}, f32[10,66,130]{2,0,1:T(8,128)}, f32[10,66,130]{2,0,1:T(8,128)}) fusion(f32[10,66,130]{2,0,1:T(8,128)} %get-tuple-element.38, f32[10,66,130]{2,0,1:T(8,128)} %get-tuple-element.34, f32[10,66,130]{2,0,1:T(8,128)} %get-tuple-element.37, ...), kind=kLoop, calls=%fused_computation.57 | loop fusion | flops 1115400 | bytes 3432000 | tf_op jit(solution)/shard_map/add | solution.py:59
  173.1 5.2 fusion.11
  178.5 39.4 %all-reduce.10 = (f32[]{:T(128)}, f32[]{:T(128)}, f32[256]{0:T(256)}) all-reduce(f32[]{:T(128)} %get-tuple-element.7, f32[]{:T(128)} %get-tuple-element.6, f32[256]{0:T(256)S(1)} %bitcast.150), channel_id=1, replica_groups=mesh['gx'=4,'gy'=4,'gz'=2] {'gx','gy','gz'}, use_global_device_ids=true, to_apply=%region_2.3 | all-reduce | flops 258 | bytes 2064 | tf_op jit(solution)/shard_map/psum | solution.py:124
  230.0 12.2 %all-reduce.5 = f32[256]{0:T(256)} all-reduce(f32[256]{0:T(256)} %dynamic-update-slice.1), channel_id=1, replica_groups=mesh['gx'=4,'gy'=4,'gz'=2] {'gx'}, use_global_device_ids=true, to_apply=%add.5 | all-reduce | flops 256 | bytes 2048
  261.4 7.9 %multiply_add_fusion.2 = (f32[10,66,130]{2,0,1:T(8,128)}, f32[10,66,130]{2,0,1:T(8,128)}, f32[10,66,130]{2,0,1:T(8,128)}, f32[10,66,130]{2,0,1:T(8,128)}) fusion(f32[10,66,130]{2,0,1:T(8,128)} %get-tuple-element.38, f32[10,66,130]{2,0,1:T(8,128)} %get-tuple-element.67, f32[10,66,130]{2,0,1:T(8,128)S(1)} %copy-done.8, f32[10,66,130]{2,0,1:T(8,128)S(1)} %copy-done.5, ...), kind=kLoop, calls=%fused_computation.49 | loop fusion | flops 1115400 | bytes 3432000 | tf_op jit(solution)/shard_map/add | solution.py:59
  269.3 5.9 multiply_reduce_fusion.5
  275.1 38.5 %psum.88 = f32[]{:T(128)} all-reduce(f32[]{:T(128)} %get-tuple-element.25), channel_id=1, replica_groups=mesh['gx'=4,'gy'=4,'gz'=2] {'gx','gy','gz'}, use_global_device_ids=true, to_apply=%region_7.8 | all-reduce | flops 1 | bytes 8 | tf_op jit(solution)/shard_map/psum | solution.py:124
  344.3 5.2 fusion.14
  350.3 39.3 %all-reduce.9 = (f32[]{:T(128)}, f32[256]{0:T(256)}) all-reduce(f32[]{:T(128)} %get-tuple-element.23, f32[256]{0:T(256)} %bitcast.161), channel_id=1, replica_groups=mesh['gx'=4,'gy'=4,'gz'=2] {'gx','gy','gz'}, use_global_device_ids=true, to_apply=%region_9.10 | all-reduce | flops 257 | bytes 2056 | tf_op jit(solution)/shard_map/psum | solution.py:136
  401.9 11.7 %all-reduce.6 = f32[256]{0:T(256)S(1)} all-reduce(f32[256]{0:T(256)} %dynamic-update-slice.2), channel_id=1, replica_groups=mesh['gx'=4,'gy'=4,'gz'=2] {'gx'}, use_global_device_ids=true, to_apply=%add.6 | all-reduce | flops 256 | bytes 2048
  434.4 7.9 %multiply_add_fusion.1 = (f32[10,66,130]{2,0,1:T(8,128)}, f32[10,66,130]{2,0,1:T(8,128)}, f32[10,66,130]{2,0,1:T(8,128)}, f32[10,66,130]{2,0,1:T(8,128)}) fusion(f32[10,66,130]{2,0,1:T(8,128)} %get-tuple-element.38, f32[10,66,130]{2,0,1:T(8,128)} %get-tuple-element.65, f32[10,66,130]{2,0,1:T(8,128)S(1)} %copy-done.9, f32[10,66,130]{2,0,1:T(8,128)S(1)} %copy-done.6, ...), kind=kLoop, calls=%fused_computation.41 | loop fusion | flops 1115400 | bytes 3432000 | tf_op jit(solution)/shard_map/add | solution.py:59
  442.3 5.9 multiply_reduce_fusion.3
  448.1 38.5 %psum.91 = f32[]{:T(128)} all-reduce(f32[]{:T(128)} %get-tuple-element.21), channel_id=1, replica_groups=mesh['gx'=4,'gy'=4,'gz'=2] {'gx','gy','gz'}, use_global_device_ids=true, to_apply=%region_12.13 | all-reduce | flops 1 | bytes 8 | tf_op jit(solution)/shard_map/psum | solution.py:124
  517.2 5.2 fusion.17
  523.2 39.3 %all-reduce.8 = (f32[]{:T(128)}, f32[256]{0:T(256)}) all-reduce(f32[]{:T(128)} %get-tuple-element.19, f32[256]{0:T(256)} %bitcast.162), channel_id=1, replica_groups=mesh['gx'=4,'gy'=4,'gz'=2] {'gx','gy','gz'}, use_global_device_ids=true, to_apply=%region_14.15 | all-reduce | flops 257 | bytes 2056 | tf_op jit(solution)/shard_map/psum | solution.py:136
  574.3 11.7 %all-reduce.7 = f32[256]{0:T(256)S(1)} all-reduce(f32[256]{0:T(256)} %dynamic-update-slice.3), channel_id=1, replica_groups=mesh['gx'=4,'gy'=4,'gz'=2] {'gx'}, use_global_device_ids=true, to_apply=%add.7 | all-reduce | flops 256 | bytes 2048
  616.4 38.4 %psum.94 = f32[]{:T(128)} all-reduce(f32[]{:T(128)} %get-tuple-element.17), channel_id=1, replica_groups=mesh['gx'=4,'gy'=4,'gz'=2] {'gx','gy','gz'}, use_global_device_ids=true, to_apply=%region_17.18 | all-reduce | flops 1 | bytes 8 | tf_op jit(solution)/shard_map/psum | solution.py:124
  685.0 39.2 %psum.95 = f32[]{:T(128)} all-reduce(f32[]{:T(128)} %get-tuple-element.15), channel_id=1, replica_groups=mesh['gx'=4,'gy'=4,'gz'=2] {'gx','gy','gz'}, use_global_device_ids=true, to_apply=%region_19.20 | all-reduce | flops 1 | bytes 8 | tf_op jit(solution)/shard_map/psum | solution.py:136
  (348 shorter events, 276.1 us)
Async XLA Ops:
  2.1 91.0 %collective-permute-start = (f32[2,8,2,128]{3,1,2,0:T(8,128)S(1)}, f32[2,8,2,128]{3,1,2,0:T(8,128)S(1)}, u32[]{:S(2)}, u32[]{:S(2)}) collective-permute-start(f32[2,8,2,128]{3,1,2,0:T(8,128)S(1)} %get-tuple-element.86), channel_id=1, source_target_pairs={{0,8},{8,16},{16,24},{1,9},{9,17},{17,25},{2,10},{10,18},{18,26},{... | collective-permute-start | bytes 49160 | tf_op jit(solution)/shard_map/ppermute | solution.py:19
  6.9 86.1 %collective-permute-start.1 = (f32[2,8,2,128]{3,1,2,0:T(8,128)S(1)}, f32[2,8,2,128]{3,1,2,0:T(8,128)S(1)}, u32[]{:S(2)}, u32[]{:S(2)}) collective-permute-start(f32[2,8,2,128]{3,1,2,0:T(8,128)S(1)} %get-tuple-element.87), channel_id=1, source_target_pairs={{8,0},{16,8},{24,16},{9,1},{17,9},{25,17},{10,2},{18,10},{26,18},{... | collective-permute-start | bytes 49160 | tf_op jit(solution)/shard_map/ppermute | solution.py:21
  8.3 78.2 %collective-permute-start.6 = (f32[8,1,128]{2,0,1:T(8,128)S(1)}, f32[8,1,128]{2,0,1:T(8,128)S(1)}, u32[]{:S(2)}, u32[]{:S(2)}) collective-permute-start(f32[8,1,128]{2,0,1:T(8,128)S(1)} %copy.93), channel_id=1, source_target_pairs={{0,8},{8,16},{16,24},{1,9},{9,17},{17,25},{2,10},{10,18},{18,26},{... | collective-permute-start | bytes 12296 | tf_op jit(solution)/shard_map/ppermute | solution.py:19
  12.8 73.8 %collective-permute-start.7 = (f32[8,1,128]{2,0,1:T(8,128)S(1)}, f32[8,1,128]{2,0,1:T(8,128)S(1)}, u32[]{:S(2)}, u32[]{:S(2)}) collective-permute-start(f32[8,1,128]{2,0,1:T(8,128)S(1)} %copy.94), channel_id=1, source_target_pairs={{8,0},{16,8},{24,16},{9,1},{17,9},{25,17},{10,2},{18,10},{26,18},{... | collective-permute-start | bytes 12296 | tf_op jit(solution)/shard_map/ppermute | solution.py:21
  87.6 16.3 %collective-permute-start.8 = (f32[8,66,1]{2,0,1:T(8,128)}, f32[8,66,1]{2,0,1:T(8,128)}, u32[]{:S(2)}, u32[]{:S(2)}) collective-permute-start(f32[8,66,1]{2,0,1:T(8,128)} %get-tuple-element.102), channel_id=1, source_target_pairs={{0,2},{2,4},{4,6},{1,3},{3,5},{5,7},{8,10},{10,12},{12,14},{9,11},... | collective-permute-start | bytes 6344 | tf_op jit(solution)/shard_map/ppermute | solution.py:19
  91.7 12.2 %collective-permute-start.9 = (f32[8,66,1]{2,0,1:T(8,128)}, f32[8,66,1]{2,0,1:T(8,128)}, u32[]{:S(2)}, u32[]{:S(2)}) collective-permute-start(f32[8,66,1]{2,0,1:T(8,128)} %get-tuple-element.103), channel_id=1, source_target_pairs={{2,0},{4,2},{6,4},{3,1},{5,3},{7,5},{10,8},{12,10},{14,12},{11,9},... | collective-permute-start | bytes 6344 | tf_op jit(solution)/shard_map/ppermute | solution.py:21
  95.5 13.9 %collective-permute-start.2 = (f32[2,8,68,2]{2,1,3,0:T(8,128)S(1)}, f32[2,8,68,2]{2,1,3,0:T(8,128)}, u32[]{:S(2)}, u32[]{:S(2)}) collective-permute-start(f32[2,8,68,2]{2,1,3,0:T(8,128)S(1)} %copy.24), channel_id=1, source_target_pairs={{0,2},{2,4},{4,6},{1,3},{3,5},{5,7},{8,10},{10,12},{12,14},{9,11},... | collective-permute-start | bytes 26120 | tf_op jit(solution)/shard_map/ppermute | solution.py:19
  106.3 13.6 %collective-permute-start.10 = (f32[1,66,130]{2,0,1:T(1,128)}, f32[1,66,130]{2,0,1:T(1,128)}, u32[]{:S(2)}, u32[]{:S(2)}) collective-permute-start(f32[1,66,130]{2,0,1:T(1,128)} %get-tuple-element.82), channel_id=1, source_target_pairs={{0,1},{2,3},{4,5},{6,7},{8,9},{10,11},{12,13},{14,15},{16,17},{18,... | collective-permute-start | bytes 102968 | tf_op jit(solution)/shard_map/ppermute | solution.py:19
  108.2 11.7 %collective-permute-start.11 = (f32[1,66,130]{2,0,1:T(1,128)}, f32[1,66,130]{2,0,1:T(1,128)}, u32[]{:S(2)}, u32[]{:S(2)}) collective-permute-start(f32[1,66,130]{2,0,1:T(1,128)} %get-tuple-element.83), channel_id=1, source_target_pairs={{1,0},{3,2},{5,4},{7,6},{9,8},{11,10},{13,12},{15,14},{17,16},{19,... | collective-permute-start | bytes 102968 | tf_op jit(solution)/shard_map/ppermute | solution.py:21
  114.5 8.1 %collective-permute-start.4 = (f32[2,2,68,132]{3,1,2,0:T(2,128)S(1)}, f32[2,2,68,132]{3,1,2,0:T(2,128)S(1)}, u32[]{:S(2)}, u32[]{:S(2)}) collective-permute-start(f32[2,2,68,132]{3,1,2,0:T(2,128)S(1)} %get-tuple-element.44), channel_id=1, source_target_pairs={{0,1},{2,3},{4,5},{6,7},{8,9},{10,11},{12,13},{14,15},{16,17},{18,... | collective-permute-start | bytes 430856 | tf_op jit(solution)/shard_map/ppermute | solution.py:19
  150.4 10.6 %collective-permute-start.14 = (f32[8,66,1]{2,0,1:T(8,128)S(1)}, f32[8,66,1]{2,0,1:T(8,128)S(1)}, u32[]{:S(2)}, u32[]{:S(2)}) collective-permute-start(f32[8,66,1]{2,0,1:T(8,128)S(1)} %get-tuple-element.100), channel_id=1, source_target_pairs={{0,2},{2,4},{4,6},{1,3},{3,5},{5,7},{8,10},{10,12},{12,14},{9,11},... | collective-permute-start | bytes 6344 | tf_op jit(solution)/shard_map/ppermute | solution.py:19
  154.9 10.1 %collective-permute-start.15 = (f32[8,66,1]{2,0,1:T(8,128)S(1)}, f32[8,66,1]{2,0,1:T(8,128)S(1)}, u32[]{:S(2)}, u32[]{:S(2)}) collective-permute-start(f32[8,66,1]{2,0,1:T(8,128)S(1)} %get-tuple-element.101), channel_id=1, source_target_pairs={{2,0},{4,2},{6,4},{3,1},{5,3},{7,5},{10,8},{12,10},{14,12},{11,9},... | collective-permute-start | bytes 6344 | tf_op jit(solution)/shard_map/ppermute | solution.py:21
  221.1 21.0 %collective-permute-start.18 = (f32[8,1,128]{2,0,1:T(8,128)}, f32[8,1,128]{2,0,1:T(8,128)S(1)}, u32[]{:S(2)}, u32[]{:S(2)}) collective-permute-start(f32[8,1,128]{2,0,1:T(8,128)} %get-tuple-element.114), channel_id=1, source_target_pairs={{0,8},{8,16},{16,24},{1,9},{9,17},{17,25},{2,10},{10,18},{18,26},{... | collective-permute-start | bytes 12296 | tf_op jit(solution)/shard_map/ppermute | solution.py:19
  225.3 16.8 %collective-permute-start.19 = (f32[8,1,128]{2,0,1:T(8,128)}, f32[8,1,128]{2,0,1:T(8,128)S(1)}, u32[]{:S(2)}, u32[]{:S(2)}) collective-permute-start(f32[8,1,128]{2,0,1:T(8,128)} %get-tuple-element.115), channel_id=1, source_target_pairs={{8,0},{16,8},{24,16},{9,1},{17,9},{25,17},{10,2},{18,10},{26,18},{... | collective-permute-start | bytes 12296 | tf_op jit(solution)/shard_map/ppermute | solution.py:21
  245.9 8.4 %collective-permute-start.21 = (f32[8,66,1]{2,0,1:T(8,128)S(1)}, f32[8,66,1]{2,0,1:T(8,128)S(1)}, u32[]{:S(2)}, u32[]{:S(2)}) collective-permute-start(f32[8,66,1]{2,0,1:T(8,128)S(1)} %get-tuple-element.99), channel_id=1, source_target_pairs={{2,0},{4,2},{6,4},{3,1},{5,3},{7,5},{10,8},{12,10},{14,12},{11,9},... | collective-permute-start | bytes 6344 | tf_op jit(solution)/shard_map/ppermute | solution.py:21
  329.4 8.4 %collective-permute-start.27 = (f32[8,66,1]{2,0,1:T(8,128)S(1)}, f32[8,66,1]{2,0,1:T(8,128)S(1)}, u32[]{:S(2)}, u32[]{:S(2)}) collective-permute-start(f32[8,66,1]{2,0,1:T(8,128)S(1)} %get-tuple-element.97), channel_id=1, source_target_pairs={{2,0},{4,2},{6,4},{3,1},{5,3},{7,5},{10,8},{12,10},{14,12},{11,9},... | collective-permute-start | bytes 6344 | tf_op jit(solution)/shard_map/ppermute | solution.py:21
  393.3 20.4 %collective-permute-start.30 = (f32[8,1,128]{2,0,1:T(8,128)}, f32[8,1,128]{2,0,1:T(8,128)S(1)}, u32[]{:S(2)}, u32[]{:S(2)}) collective-permute-start(f32[8,1,128]{2,0,1:T(8,128)} %get-tuple-element.110), channel_id=1, source_target_pairs={{0,8},{8,16},{16,24},{1,9},{9,17},{17,25},{2,10},{10,18},{18,26},{... | collective-permute-start | bytes 12296 | tf_op jit(solution)/shard_map/ppermute | solution.py:19
  397.4 16.3 %collective-permute-start.31 = (f32[8,1,128]{2,0,1:T(8,128)}, f32[8,1,128]{2,0,1:T(8,128)S(1)}, u32[]{:S(2)}, u32[]{:S(2)}) collective-permute-start(f32[8,1,128]{2,0,1:T(8,128)} %get-tuple-element.111), channel_id=1, source_target_pairs={{8,0},{16,8},{24,16},{9,1},{17,9},{25,17},{10,2},{18,10},{26,18},{... | collective-permute-start | bytes 12296 | tf_op jit(solution)/shard_map/ppermute | solution.py:21
  418.2 8.4 %collective-permute-start.33 = (f32[8,66,1]{2,0,1:T(8,128)S(1)}, f32[8,66,1]{2,0,1:T(8,128)S(1)}, u32[]{:S(2)}, u32[]{:S(2)}) collective-permute-start(f32[8,66,1]{2,0,1:T(8,128)S(1)} %get-tuple-element.95), channel_id=1, source_target_pairs={{2,0},{4,2},{6,4},{3,1},{5,3},{7,5},{10,8},{12,10},{14,12},{11,9},... | collective-permute-start | bytes 6344 | tf_op jit(solution)/shard_map/ppermute | solution.py:21
  502.4 8.4 %collective-permute-start.39 = (f32[8,66,1]{2,0,1:T(8,128)S(1)}, f32[8,66,1]{2,0,1:T(8,128)S(1)}, u32[]{:S(2)}, u32[]{:S(2)}) collective-permute-start(f32[8,66,1]{2,0,1:T(8,128)S(1)} %get-tuple-element.93), channel_id=1, source_target_pairs={{2,0},{4,2},{6,4},{3,1},{5,3},{7,5},{10,8},{12,10},{14,12},{11,9},... | collective-permute-start | bytes 6344 | tf_op jit(solution)/shard_map/ppermute | solution.py:21
  566.1 19.9 %collective-permute-start.42 = (f32[8,1,128]{2,0,1:T(8,128)}, f32[8,1,128]{2,0,1:T(8,128)S(1)}, u32[]{:S(2)}, u32[]{:S(2)}) collective-permute-start(f32[8,1,128]{2,0,1:T(8,128)} %get-tuple-element.106), channel_id=1, source_target_pairs={{0,8},{8,16},{16,24},{1,9},{9,17},{17,25},{2,10},{10,18},{18,26},{... | collective-permute-start | bytes 12296 | tf_op jit(solution)/shard_map/ppermute | solution.py:19
  570.2 15.8 %collective-permute-start.43 = (f32[8,1,128]{2,0,1:T(8,128)}, f32[8,1,128]{2,0,1:T(8,128)S(1)}, u32[]{:S(2)}, u32[]{:S(2)}) collective-permute-start(f32[8,1,128]{2,0,1:T(8,128)} %get-tuple-element.107), channel_id=1, source_target_pairs={{8,0},{16,8},{24,16},{9,1},{17,9},{25,17},{10,2},{18,10},{26,18},{... | collective-permute-start | bytes 12296 | tf_op jit(solution)/shard_map/ppermute | solution.py:21
  590.5 8.4 %collective-permute-start.45 = (f32[8,66,1]{2,0,1:T(8,128)S(1)}, f32[8,66,1]{2,0,1:T(8,128)S(1)}, u32[]{:S(2)}, u32[]{:S(2)}) collective-permute-start(f32[8,66,1]{2,0,1:T(8,128)S(1)} %get-tuple-element.91), channel_id=1, source_target_pairs={{2,0},{4,2},{6,4},{3,1},{5,3},{7,5},{10,8},{12,10},{14,12},{11,9},... | collective-permute-start | bytes 6344 | tf_op jit(solution)/shard_map/ppermute | solution.py:21
  669.6 8.4 %collective-permute-start.51 = (f32[8,66,1]{2,0,1:T(8,128)S(1)}, f32[8,66,1]{2,0,1:T(8,128)S(1)}, u32[]{:S(2)}, u32[]{:S(2)}) collective-permute-start(f32[8,66,1]{2,0,1:T(8,128)S(1)} %get-tuple-element.89), channel_id=1, source_target_pairs={{2,0},{4,2},{6,4},{3,1},{5,3},{7,5},{10,8},{12,10},{14,12},{11,9},... | collective-permute-start | bytes 6344 | tf_op jit(solution)/shard_map/ppermute | solution.py:21
  (100 other events, 1150.4 us)
where the time goes:
time: 739 us; the launch traced here: 728 us
  blocking collectives  361 us (49%)
  starting transfers between devices  121 us (16%)
  other arithmetic  90.9 us (12%)
  waiting for transfers between devices  73.3 us (10%)
  matrix products  37.2 us (5%)
  local copies, waits for them, and re-layouts  27.4 us (4%)
  between operations  16.1 us (2%)
    psum x4, blocking collectives, inner_of(): return lax.psum(jnp.sum(residual * precond), ('gx', 'gy', 'gz'))  155 us
    psum x3, blocking collectives, local(): lax.psum((jnp.sum(direction * applied), coarse_terms(applied)), ('gx', 'g...  118 us
    ppermute x27, starting transfers between devices, padded_2(): lax.ppermute(tail, axis, [(i, (i + 1) % count) for i in range(ends)])  85 us
    ppermute x27, waiting for transfers between devices, padded_2(): lax.ppermute(head, axis, [((i + 1) % count, i) for i in range(ends)])  55.2 us
    unnamed x4, blocking collectives  46.7 us
    psum x1, blocking collectives, local(): vector = lax.psum(coarse_terms(residual), ('gx', 'gy', 'gz'))  42 us
    ppermute x27, starting transfers between devices, padded_2(): lax.ppermute(head, axis, [((i + 1) % count, i) for i in range(ends)])  36.3 us
    add x4, other arithmetic, stencil(): applied + transmit * (center - neighbour(padded, dimension, offset))  28.6 us
  transfers between devices with their start and end apart: 54, of which 22 were waited for; matrix products, arithmetic and copies ran while one was open for 7% of the time, Pallas kernels for 0%

commit v1 on v0

--- a/solution.py
+++ b/solution.py
@@ -126,7 +126,9 @@
     solution = jnp.zeros(right_side.shape, jnp.float32)
     residual = right_side
     residual_ext = residual_rim(residual)
-    vector = lax.psum(coarse_terms(residual), ("gx", "gy", "gz"))
+    vector = coarse_terms(residual)
+    for mesh_axis in (("gy", "gz"), "gx"):
+        vector = lax.psum(vector, mesh_axis)
     precond = precondition(residual_ext, vector)
     inner_prod = inner_of(residual, precond)
     direction = precond

time: 739 us -> 724 us (0.980)
  blocking collectives: 361 us -> 344 us
    psum x1 -> x2, blocking collectives: 42 us -> 26.5 us  [local(): vector = lax.psum(vector, mesh_axis)]
where the time goes in v1:
time: 724 us; the launch traced here: 713 us
  blocking collectives  344 us (48%)
  starting transfers between devices  120 us (17%)
  other arithmetic  92.6 us (13%)
  waiting for transfers between devices  72.7 us (10%)
  matrix products  37.4 us (5%)
  local copies, waits for them, and re-layouts  29.2 us (4%)
  between operations  16.7 us (2%)
    psum x4, blocking collectives, inner_of(): return lax.psum(jnp.sum(residual * precond), ('gx', 'gy', 'gz'))  155 us
    psum x3, blocking collectives, local(): lax.psum((jnp.sum(direction * applied), coarse_terms(applied)), ('gx', 'g...  118 us
    ppermute x27, starting transfers between devices, padded_2(): lax.ppermute(tail, axis, [(i, (i + 1) % count) for i in range(ends)])  83.7 us
    ppermute x27, waiting for transfers between devices, padded_2(): lax.ppermute(head, axis, [((i + 1) % count, i) for i in range(ends)])  54.6 us
    unnamed x4, blocking collectives  44.8 us
    ppermute x27, starting transfers between devices, padded_2(): lax.ppermute(head, axis, [((i + 1) % count, i) for i in range(ends)])  36.3 us
    add x4, other arithmetic, stencil(): applied + transmit * (center - neighbour(padded, dimension, offset))  31.4 us
    psum x2, blocking collectives, local(): vector = lax.psum(vector, mesh_axis)  26.5 us
  transfers between devices with their start and end apart: 54, of which 22 were waited for; matrix products, arithmetic and copies ran while one was open for 7% of the time, Pallas kernels for 0%

profile of v1, /device:TPU:0, one launch (start us, length us, event | category | flops | bytes accessed | tf_op | source)
XLA Modules:
  0.0 712.7 jit_solution(421256332715025427)
XLA Ops:
  2.7 5.5 collective-permute-start
  17.9 6.5 fusion.8
  24.6 15.8 %psum.91 = f32[256]{0:T(256)S(1)} all-reduce(f32[256]{0:T(256)S(1)} %bitcast.151), channel_id=1, replica_groups=mesh['gx'=4,'gy'=4,'gz'=2] {'gy','gz'}, use_global_device_ids=true, to_apply=%region_0.1 | all-reduce | flops 256 | bytes 2048 | tf_op jit(solution)/shard_map/psum | solution.py:131
  40.4 10.8 %psum.92 = f32[256]{0:T(256)S(1)} all-reduce(f32[256]{0:T(256)S(1)} %psum.91), channel_id=1, replica_groups=mesh['gx'=4,'gy'=4,'gz'=2] {'gx'}, use_global_device_ids=true, to_apply=%region_1.2 | all-reduce | flops 256 | bytes 2048 | tf_op jit(solution)/shard_map/psum | solution.py:131
  52.8 9.2 %all-reduce.4 = f32[256]{0:T(256)S(1)} all-reduce(f32[256]{0:T(256)S(1)} %dynamic-update-slice), channel_id=1, replica_groups=mesh['gx'=4,'gy'=4,'gz'=2] {'gx'}, use_global_device_ids=true, to_apply=%add.4 | all-reduce | flops 256 | bytes 2048
  106.9 5.7 fusion.144
  112.6 8.2 %multiply_add_fusion.3 = (f32[10,66,130]{2,0,1:T(8,128)}, f32[10,66,130]{2,0,1:T(8,128)}, f32[10,66,130]{2,0,1:T(8,128)}, f32[10,66,130]{2,0,1:T(8,128)}) fusion(f32[10,66,130]{2,0,1:T(8,128)} %get-tuple-element.38, f32[10,66,130]{2,0,1:T(8,128)} %get-tuple-element.34, f32[10,66,130]{2,0,1:T(8,128)S(1)} %get-tuple-element.37, ...), kind=kLoop, calls=%fused_computation.57 | loop fusion | flops 1115400 | bytes 3432000 | tf_op jit(solution)/shard_map/add | solution.py:59
  155.8 5.2 fusion.11
  161.3 39.1 %all-reduce.10 = (f32[]{:T(128)}, f32[]{:T(128)}, f32[256]{0:T(256)}) all-reduce(f32[]{:T(128)} %get-tuple-element.7, f32[]{:T(128)} %get-tuple-element.6, f32[256]{0:T(256)S(1)} %bitcast.150), channel_id=1, replica_groups=mesh['gx'=4,'gy'=4,'gz'=2] {'gx','gy','gz'}, use_global_device_ids=true, to_apply=%region_3.4 | all-reduce | flops 258 | bytes 2064 | tf_op jit(solution)/shard_map/psum | solution.py:124
  212.2 12.1 %all-reduce.5 = f32[256]{0:T(256)} all-reduce(f32[256]{0:T(256)} %dynamic-update-slice.1), channel_id=1, replica_groups=mesh['gx'=4,'gy'=4,'gz'=2] {'gx'}, use_global_device_ids=true, to_apply=%add.5 | all-reduce | flops 256 | bytes 2048
  244.8 7.9 %multiply_add_fusion.2 = (f32[10,66,130]{2,0,1:T(8,128)}, f32[10,66,130]{2,0,1:T(8,128)}, f32[10,66,130]{2,0,1:T(8,128)}, f32[10,66,130]{2,0,1:T(8,128)}) fusion(f32[10,66,130]{2,0,1:T(8,128)S(1)} %copy-done.12, f32[10,66,130]{2,0,1:T(8,128)} %get-tuple-element.67, f32[10,66,130]{2,0,1:T(8,128)S(1)} %copy-done.9, f32[10,66,130]{2,0,1:T(8,128)S(1)} %copy-done.5, ...), kind=kLoop, calls=%fused_computation.49 | loop fusion | flops 1115400 | bytes 3432000 | tf_op jit(solution)/shard_map/add | solution.py:59
  252.7 5.9 multiply_reduce_fusion.5
  258.6 38.5 %psum.96 = f32[]{:T(128)} all-reduce(f32[]{:T(128)} %get-tuple-element.25), channel_id=1, replica_groups=mesh['gx'=4,'gy'=4,'gz'=2] {'gx','gy','gz'}, use_global_device_ids=true, to_apply=%region_8.9 | all-reduce | flops 1 | bytes 8 | tf_op jit(solution)/shard_map/psum | solution.py:124
  333.8 39.3 %all-reduce.9 = (f32[]{:T(128)}, f32[256]{0:T(256)}) all-reduce(f32[]{:T(128)} %get-tuple-element.23, f32[256]{0:T(256)} %bitcast.161), channel_id=1, replica_groups=mesh['gx'=4,'gy'=4,'gz'=2] {'gx','gy','gz'}, use_global_device_ids=true, to_apply=%region_10.11 | all-reduce | flops 257 | bytes 2056 | tf_op jit(solution)/shard_map/psum | solution.py:138
  385.7 11.7 %all-reduce.6 = f32[256]{0:T(256)S(1)} all-reduce(f32[256]{0:T(256)} %dynamic-update-slice.2), channel_id=1, replica_groups=mesh['gx'=4,'gy'=4,'gz'=2] {'gx'}, use_global_device_ids=true, to_apply=%add.6 | all-reduce | flops 256 | bytes 2048
  418.4 7.9 %multiply_add_fusion.1 = (f32[10,66,130]{2,0,1:T(8,128)}, f32[10,66,130]{2,0,1:T(8,128)}, f32[10,66,130]{2,0,1:T(8,128)}, f32[10,66,130]{2,0,1:T(8,128)}) fusion(f32[10,66,130]{2,0,1:T(8,128)S(1)} %copy-done.13, f32[10,66,130]{2,0,1:T(8,128)} %get-tuple-element.65, f32[10,66,130]{2,0,1:T(8,128)S(1)} %copy-done.10, f32[10,66,130]{2,0,1:T(8,128)S(1)} %copy-done.6, ...), kind=kLoop, calls=%fused_computation.41 | loop fusion | flops 1115400 | bytes 3432000 | tf_op jit(solution)/shard_map/add | solution.py:59
  426.3 5.9 multiply_reduce_fusion.3
  432.2 38.7 %psum.99 = f32[]{:T(128)} all-reduce(f32[]{:T(128)} %get-tuple-element.21), channel_id=1, replica_groups=mesh['gx'=4,'gy'=4,'gz'=2] {'gx','gy','gz'}, use_global_device_ids=true, to_apply=%region_13.14 | all-reduce | flops 1 | bytes 8 | tf_op jit(solution)/shard_map/psum | solution.py:124
  501.4 5.2 fusion.17
  506.8 39.3 %all-reduce.8 = (f32[]{:T(128)}, f32[256]{0:T(256)}) all-reduce(f32[]{:T(128)} %get-tuple-element.19, f32[256]{0:T(256)S(1)} %bitcast.162), channel_id=1, replica_groups=mesh['gx'=4,'gy'=4,'gz'=2] {'gx','gy','gz'}, use_global_device_ids=true, to_apply=%region_15.16 | all-reduce | flops 257 | bytes 2056 | tf_op jit(solution)/shard_map/psum | solution.py:138
  557.3 11.7 %all-reduce.7 = f32[256]{0:T(256)S(1)} all-reduce(f32[256]{0:T(256)} %dynamic-update-slice.3), channel_id=1, replica_groups=mesh['gx'=4,'gy'=4,'gz'=2] {'gx'}, use_global_device_ids=true, to_apply=%add.7 | all-reduce | flops 256 | bytes 2048
  589.3 7.4 %multiply_add_fusion = (f32[10,66,130]{2,0,1:T(8,128)}, f32[10,66,130]{2,0,1:T(8,128)}, f32[10,66,130]{2,0,1:T(8,128)}, f32[10,66,130]{2,0,1:T(8,128)}) fusion(f32[10,66,130]{2,0,1:T(8,128)S(1)} %copy-done.14, f32[10,66,130]{2,0,1:T(8,128)} %get-tuple-element.63, f32[10,66,130]{2,0,1:T(8,128)S(1)} %copy-done.11, f32[10,66,130]{2,0,1:T(8,128)S(1)} %copy-done.7, ...), kind=kLoop, calls=%fused_computation.33 | loop fusion | flops 1115400 | bytes 3432000 | tf_op jit(solution)/shard_map/add | solution.py:59
  601.8 38.5 %psum.102 = f32[]{:T(128)} all-reduce(f32[]{:T(128)} %get-tuple-element.17), channel_id=1, replica_groups=mesh['gx'=4,'gy'=4,'gz'=2] {'gx','gy','gz'}, use_global_device_ids=true, to_apply=%region_18.19 | all-reduce | flops 1 | bytes 8 | tf_op jit(solution)/shard_map/psum | solution.py:124
  669.9 39.3 %psum.103 = f32[]{:T(128)} all-reduce(f32[]{:T(128)} %get-tuple-element.15), channel_id=1, replica_groups=mesh['gx'=4,'gy'=4,'gz'=2] {'gx','gy','gz'}, use_global_device_ids=true, to_apply=%region_20.21 | all-reduce | flops 1 | bytes 8 | tf_op jit(solution)/shard_map/psum | solution.py:138
  (381 shorter events, 280.6 us)
Async XLA Ops:
  2.7 70.6 %collective-permute-start = (f32[2,8,2,128]{3,1,2,0:T(8,128)}, f32[2,8,2,128]{3,1,2,0:T(8,128)}, u32[]{:S(2)}, u32[]{:S(2)}) collective-permute-start(f32[2,8,2,128]{3,1,2,0:T(8,128)} %get-tuple-element.86), channel_id=1, source_target_pairs={{0,8},{8,16},{16,24},{1,9},{9,17},{17,25},{2,10},{10,18},{18,26},{... | collective-permute-start | bytes 49160 | tf_op jit(solution)/shard_map/ppermute | solution.py:19
  8.1 65.2 %collective-permute-start.1 = (f32[2,8,2,128]{3,1,2,0:T(8,128)}, f32[2,8,2,128]{3,1,2,0:T(8,128)}, u32[]{:S(2)}, u32[]{:S(2)}) collective-permute-start(f32[2,8,2,128]{3,1,2,0:T(8,128)} %get-tuple-element.87), channel_id=1, source_target_pairs={{8,0},{16,8},{24,16},{9,1},{17,9},{25,17},{10,2},{18,10},{26,18},{... | collective-permute-start | bytes 49160 | tf_op jit(solution)/shard_map/ppermute | solution.py:21
  9.4 60.1 %collective-permute-start.6 = (f32[8,1,128]{2,0,1:T(8,128)S(1)}, f32[8,1,128]{2,0,1:T(8,128)S(1)}, u32[]{:S(2)}, u32[]{:S(2)}) collective-permute-start(f32[8,1,128]{2,0,1:T(8,128)S(1)} %copy.93), channel_id=1, source_target_pairs={{0,8},{8,16},{16,24},{1,9},{9,17},{17,25},{2,10},{10,18},{18,26},{... | collective-permute-start | bytes 12296 | tf_op jit(solution)/shard_map/ppermute | solution.py:19
  14.0 55.7 %collective-permute-start.7 = (f32[8,1,128]{2,0,1:T(8,128)S(1)}, f32[8,1,128]{2,0,1:T(8,128)S(1)}, u32[]{:S(2)}, u32[]{:S(2)}) collective-permute-start(f32[8,1,128]{2,0,1:T(8,128)S(1)} %copy.94), channel_id=1, source_target_pairs={{8,0},{16,8},{24,16},{9,1},{17,9},{25,17},{10,2},{18,10},{26,18},{... | collective-permute-start | bytes 12296 | tf_op jit(solution)/shard_map/ppermute | solution.py:21
  70.7 14.8 %collective-permute-start.8 = (f32[8,66,1]{2,0,1:T(8,128)}, f32[8,66,1]{2,0,1:T(8,128)S(1)}, u32[]{:S(2)}, u32[]{:S(2)}) collective-permute-start(f32[8,66,1]{2,0,1:T(8,128)} %get-tuple-element.102), channel_id=1, source_target_pairs={{0,2},{2,4},{4,6},{1,3},{3,5},{5,7},{8,10},{10,12},{12,14},{9,11},... | collective-permute-start | bytes 6344 | tf_op jit(solution)/shard_map/ppermute | solution.py:19
  72.0 13.5 %collective-permute-start.9 = (f32[8,66,1]{2,0,1:T(8,128)}, f32[8,66,1]{2,0,1:T(8,128)S(1)}, u32[]{:S(2)}, u32[]{:S(2)}) collective-permute-start(f32[8,66,1]{2,0,1:T(8,128)} %get-tuple-element.103), channel_id=1, source_target_pairs={{2,0},{4,2},{6,4},{3,1},{5,3},{7,5},{10,8},{12,10},{14,12},{11,9},... | collective-permute-start | bytes 6344 | tf_op jit(solution)/shard_map/ppermute | solution.py:21
  77.1 12.7 %collective-permute-start.2 = (f32[2,8,68,2]{2,1,3,0:T(8,128)}, f32[2,8,68,2]{2,1,3,0:T(8,128)}, u32[]{:S(2)}, u32[]{:S(2)}) collective-permute-start(f32[2,8,68,2]{2,1,3,0:T(8,128)} %copy.24), channel_id=1, source_target_pairs={{0,2},{2,4},{4,6},{1,3},{3,5},{5,7},{8,10},{10,12},{12,14},{9,11},... | collective-permute-start | bytes 26120 | tf_op jit(solution)/shard_map/ppermute | solution.py:19
  86.7 14.7 %collective-permute-start.10 = (f32[1,66,130]{2,0,1:T(1,128)}, f32[1,66,130]{2,0,1:T(1,128)}, u32[]{:S(2)}, u32[]{:S(2)}) collective-permute-start(f32[1,66,130]{2,0,1:T(1,128)} %get-tuple-element.82), channel_id=1, source_target_pairs={{0,1},{2,3},{4,5},{6,7},{8,9},{10,11},{12,13},{14,15},{16,17},{18,... | collective-permute-start | bytes 102968 | tf_op jit(solution)/shard_map/ppermute | solution.py:19
  88.6 12.8 %collective-permute-start.11 = (f32[1,66,130]{2,0,1:T(1,128)}, f32[1,66,130]{2,0,1:T(1,128)}, u32[]{:S(2)}, u32[]{:S(2)}) collective-permute-start(f32[1,66,130]{2,0,1:T(1,128)} %get-tuple-element.83), channel_id=1, source_target_pairs={{1,0},{3,2},{5,4},{7,6},{9,8},{11,10},{13,12},{15,14},{17,16},{19,... | collective-permute-start | bytes 102968 | tf_op jit(solution)/shard_map/ppermute | solution.py:21
  96.1 7.9 %collective-permute-start.4 = (f32[2,2,68,132]{3,1,2,0:T(2,128)S(1)}, f32[2,2,68,132]{3,1,2,0:T(2,128)S(1)}, u32[]{:S(2)}, u32[]{:S(2)}) collective-permute-start(f32[2,2,68,132]{3,1,2,0:T(2,128)S(1)} %get-tuple-element.44), channel_id=1, source_target_pairs={{0,1},{2,3},{4,5},{6,7},{8,9},{10,11},{12,13},{14,15},{16,17},{18,... | collective-permute-start | bytes 430856 | tf_op jit(solution)/shard_map/ppermute | solution.py:19
  133.2 10.5 %collective-permute-start.14 = (f32[8,66,1]{2,0,1:T(8,128)S(1)}, f32[8,66,1]{2,0,1:T(8,128)S(1)}, u32[]{:S(2)}, u32[]{:S(2)}) collective-permute-start(f32[8,66,1]{2,0,1:T(8,128)S(1)} %get-tuple-element.100), channel_id=1, source_target_pairs={{0,2},{2,4},{4,6},{1,3},{3,5},{5,7},{8,10},{10,12},{12,14},{9,11},... | collective-permute-start | bytes 6344 | tf_op jit(solution)/shard_map/ppermute | solution.py:19
  137.8 10.1 %collective-permute-start.15 = (f32[8,66,1]{2,0,1:T(8,128)S(1)}, f32[8,66,1]{2,0,1:T(8,128)S(1)}, u32[]{:S(2)}, u32[]{:S(2)}) collective-permute-start(f32[8,66,1]{2,0,1:T(8,128)S(1)} %get-tuple-element.101), channel_id=1, source_target_pairs={{2,0},{4,2},{6,4},{3,1},{5,3},{7,5},{10,8},{12,10},{14,12},{11,9},... | collective-permute-start | bytes 6344 | tf_op jit(solution)/shard_map/ppermute | solution.py:21
  203.6 20.8 %collective-permute-start.18 = (f32[8,1,128]{2,0,1:T(8,128)}, f32[8,1,128]{2,0,1:T(8,128)S(1)}, u32[]{:S(2)}, u32[]{:S(2)}) collective-permute-start(f32[8,1,128]{2,0,1:T(8,128)} %get-tuple-element.114), channel_id=1, source_target_pairs={{0,8},{8,16},{16,24},{1,9},{9,17},{17,25},{2,10},{10,18},{18,26},{... | collective-permute-start | bytes 12296 | tf_op jit(solution)/shard_map/ppermute | solution.py:19
  207.8 16.6 %collective-permute-start.19 = (f32[8,1,128]{2,0,1:T(8,128)}, f32[8,1,128]{2,0,1:T(8,128)S(1)}, u32[]{:S(2)}, u32[]{:S(2)}) collective-permute-start(f32[8,1,128]{2,0,1:T(8,128)} %get-tuple-element.115), channel_id=1, source_target_pairs={{8,0},{16,8},{24,16},{9,1},{17,9},{25,17},{10,2},{18,10},{26,18},{... | collective-permute-start | bytes 12296 | tf_op jit(solution)/shard_map/ppermute | solution.py:21
  228.2 8.4 %collective-permute-start.21 = (f32[8,66,1]{2,0,1:T(8,128)S(1)}, f32[8,66,1]{2,0,1:T(8,128)S(1)}, u32[]{:S(2)}, u32[]{:S(2)}) collective-permute-start(f32[8,66,1]{2,0,1:T(8,128)S(1)} %get-tuple-element.99), channel_id=1, source_target_pairs={{2,0},{4,2},{6,4},{3,1},{5,3},{7,5},{10,8},{12,10},{14,12},{11,9},... | collective-permute-start | bytes 6344 | tf_op jit(solution)/shard_map/ppermute | solution.py:21
  312.8 8.4 %collective-permute-start.27 = (f32[8,66,1]{2,0,1:T(8,128)S(1)}, f32[8,66,1]{2,0,1:T(8,128)S(1)}, u32[]{:S(2)}, u32[]{:S(2)}) collective-permute-start(f32[8,66,1]{2,0,1:T(8,128)S(1)} %get-tuple-element.97), channel_id=1, source_target_pairs={{2,0},{4,2},{6,4},{3,1},{5,3},{7,5},{10,8},{12,10},{14,12},{11,9},... | collective-permute-start | bytes 6344 | tf_op jit(solution)/shard_map/ppermute | solution.py:21
  376.8 20.7 %collective-permute-start.30 = (f32[8,1,128]{2,0,1:T(8,128)}, f32[8,1,128]{2,0,1:T(8,128)S(1)}, u32[]{:S(2)}, u32[]{:S(2)}) collective-permute-start(f32[8,1,128]{2,0,1:T(8,128)} %get-tuple-element.110), channel_id=1, source_target_pairs={{0,8},{8,16},{16,24},{1,9},{9,17},{17,25},{2,10},{10,18},{18,26},{... | collective-permute-start | bytes 12296 | tf_op jit(solution)/shard_map/ppermute | solution.py:19
  381.1 16.4 %collective-permute-start.31 = (f32[8,1,128]{2,0,1:T(8,128)}, f32[8,1,128]{2,0,1:T(8,128)S(1)}, u32[]{:S(2)}, u32[]{:S(2)}) collective-permute-start(f32[8,1,128]{2,0,1:T(8,128)} %get-tuple-element.111), channel_id=1, source_target_pairs={{8,0},{16,8},{24,16},{9,1},{17,9},{25,17},{10,2},{18,10},{26,18},{... | collective-permute-start | bytes 12296 | tf_op jit(solution)/shard_map/ppermute | solution.py:21
  401.9 8.4 %collective-permute-start.33 = (f32[8,66,1]{2,0,1:T(8,128)S(1)}, f32[8,66,1]{2,0,1:T(8,128)S(1)}, u32[]{:S(2)}, u32[]{:S(2)}) collective-permute-start(f32[8,66,1]{2,0,1:T(8,128)S(1)} %get-tuple-element.95), channel_id=1, source_target_pairs={{2,0},{4,2},{6,4},{3,1},{5,3},{7,5},{10,8},{12,10},{14,12},{11,9},... | collective-permute-start | bytes 6344 | tf_op jit(solution)/shard_map/ppermute | solution.py:21
  486.5 8.4 %collective-permute-start.39 = (f32[8,66,1]{2,0,1:T(8,128)S(1)}, f32[8,66,1]{2,0,1:T(8,128)S(1)}, u32[]{:S(2)}, u32[]{:S(2)}) collective-permute-start(f32[8,66,1]{2,0,1:T(8,128)S(1)} %get-tuple-element.93), channel_id=1, source_target_pairs={{2,0},{4,2},{6,4},{3,1},{5,3},{7,5},{10,8},{12,10},{14,12},{11,9},... | collective-permute-start | bytes 6344 | tf_op jit(solution)/shard_map/ppermute | solution.py:21
  549.2 19.9 %collective-permute-start.42 = (f32[8,1,128]{2,0,1:T(8,128)}, f32[8,1,128]{2,0,1:T(8,128)S(1)}, u32[]{:S(2)}, u32[]{:S(2)}) collective-permute-start(f32[8,1,128]{2,0,1:T(8,128)} %get-tuple-element.106), channel_id=1, source_target_pairs={{0,8},{8,16},{16,24},{1,9},{9,17},{17,25},{2,10},{10,18},{18,26},{... | collective-permute-start | bytes 12296 | tf_op jit(solution)/shard_map/ppermute | solution.py:19
  553.3 15.7 %collective-permute-start.43 = (f32[8,1,128]{2,0,1:T(8,128)}, f32[8,1,128]{2,0,1:T(8,128)S(1)}, u32[]{:S(2)}, u32[]{:S(2)}) collective-permute-start(f32[8,1,128]{2,0,1:T(8,128)} %get-tuple-element.107), channel_id=1, source_target_pairs={{8,0},{16,8},{24,16},{9,1},{17,9},{25,17},{10,2},{18,10},{26,18},{... | collective-permute-start | bytes 12296 | tf_op jit(solution)/shard_map/ppermute | solution.py:21
  572.5 8.4 %collective-permute-start.45 = (f32[8,66,1]{2,0,1:T(8,128)S(1)}, f32[8,66,1]{2,0,1:T(8,128)S(1)}, u32[]{:S(2)}, u32[]{:S(2)}) collective-permute-start(f32[8,66,1]{2,0,1:T(8,128)S(1)} %get-tuple-element.91), channel_id=1, source_target_pairs={{2,0},{4,2},{6,4},{3,1},{5,3},{7,5},{10,8},{12,10},{14,12},{11,9},... | collective-permute-start | bytes 6344 | tf_op jit(solution)/shard_map/ppermute | solution.py:21
  655.2 8.4 %collective-permute-start.51 = (f32[8,66,1]{2,0,1:T(8,128)S(1)}, f32[8,66,1]{2,0,1:T(8,128)S(1)}, u32[]{:S(2)}, u32[]{:S(2)}) collective-permute-start(f32[8,66,1]{2,0,1:T(8,128)S(1)} %get-tuple-element.89), channel_id=1, source_target_pairs={{2,0},{4,2},{6,4},{3,1},{5,3},{7,5},{10,8},{12,10},{14,12},{11,9},... | collective-permute-start | bytes 6344 | tf_op jit(solution)/shard_map/ppermute | solution.py:21
  (116 other events, 1440.8 us)
